TPU v7x, 32 devices: a whole 2x2x4 slice. The times are simulated.
32 devices in a mesh: clip: 8 (over z, core), frame: 4 (over y, x).
Axes of the slice: x: 2, y: 2, z: 4, core: 2. Of those that a mesh axis runs over, the one named last changes fastest.
Arguments:
- block_input: bfloat16 [16, 16, 64, 1152], P('clip', 'frame'), may hold values from -6 to 6
- modulation: bfloat16 [16, 6912], P('clip'), may hold values from -4 to 4
- frame_counts: int32 [16], P('clip'), may hold values from 8 to 16, as said below
- qkv_weight: bfloat16 [1152, 3456], replicated, may hold values from -0.1875 to 0.1875
- qv_bias: bfloat16 [2304], replicated, may hold values from -3 to 3
- out_weight: bfloat16 [1152, 1152], replicated, may hold values from -0.375 to 0.375
- out_bias: bfloat16 [1152], replicated, may hold values from -3 to 3
- fc1_weight: bfloat16 [1152, 4608], replicated, may hold values from -0.1875 to 0.1875
- fc1_bias: bfloat16 [4608], replicated, may hold values from -3 to 3
- fc2_weight: bfloat16 [4608, 1152], replicated, may hold values from -0.09375 to 0.09375
- fc2_bias: bfloat16 [1152], replicated, may hold values from -3 to 3
- out_cotangent: bfloat16 [16, 16, 64, 1152], P('clip', 'frame'), may hold values from -6 to 6
Outputs:
- block_output: bfloat16 [16, 16, 64, 1152], P('clip', 'frame')
- input_grad: bfloat16 [16, 16, 64, 1152], P('clip', 'frame')
- modulation_grad: float32 [16, 6912], P('clip', 'frame')
- qkv_weight_grad: float32 [1152, 3456], P('clip', 'frame')
- qv_bias_grad: float32 [2304], P('frame')
- out_weight_grad: float32 [1152, 1152], P('clip', 'frame')
- out_bias_grad: float32 [1152], P('frame')
- fc1_weight_grad: float32 [1152, 4608], P('clip', 'frame')
- fc1_bias_grad: float32 [4608], P('frame')
- fc2_weight_grad: float32 [4608, 1152], P('clip', 'frame')
- fc2_bias_grad: float32 [1152], P('frame')
Inputs may be any that keep to these rules, and one draw needn't show every extreme that they name: `frame_counts`: each clip holds 8 to 16 frames in its leading slots; some clip holds 16 and some other clip 16 // 2.
All inputs are finite; a program needn't handle non-finite values.
Results may differ from a plain program's by a relative error of at most 0.013.
The roundings to bfloat16 on the way count: a program that leaves them out, or rounds other values in their place, can miss the bound.
Values may be sent and summed in bfloat16 or wider, within the bound.
A program may use at most 256 MiB of HBM per device.

v0:
```python
import jax
import jax.numpy as jnp
from jax import lax
from jax.sharding import PartitionSpec as P

HEADS = 16
EPSILON = 1e-06
NEGATIVE = -1e30


def normalize(values):
    centred = values - jnp.mean(values, axis=-1, keepdims=True)
    variance = jnp.mean(centred * centred, axis=-1, keepdims=True)
    return centred * lax.rsqrt(variance + EPSILON)


def modulate(values, shift_term, scale_term):
    return normalize(values) * (1.0 + scale_term) + shift_term


def gelu_tanh(inputs):
    return jax.nn.gelu(inputs, approximate=True)


def contract_rows(left, right):
    return lax.dot_general(
        left, right, (((0,), (0,)), ((), ())), preferred_element_type=jnp.float32
    )


def contract_cols(left, right):
    return lax.dot_general(
        left, right, (((1,), (1,)), ((), ())), preferred_element_type=jnp.float32
    )


def on_device(
    block_input,
    modulation,
    frame_counts,
    qkv_weight,
    qv_bias,
    out_weight,
    out_bias,
    fc1_weight,
    fc1_bias,
    fc2_weight,
    fc2_bias,
    out_cotangent,
):
    swapped = lax.all_to_all(block_input, "frame", split_axis=2, concat_axis=1, tiled=True)
    clip_count, frames, patches, model_width = swapped.shape
    head_width = model_width // HEADS
    row_count = clip_count * frames * patches
    factor = head_width ** (-0.5)
    frame_valid = (jnp.arange(frames)[None, :] < frame_counts[:, None]).astype(jnp.float32)
    valid_rows = frame_valid[:, :, None, None]
    key_valid = frame_valid[:, None, None, None, :] > 0.5
    modulators = modulation.astype(jnp.float32).reshape(clip_count, 6, model_width)[
        :, :, None, None, :
    ]
    shift_one = modulators[:, 0]
    scale_one = modulators[:, 1]
    gate_one = modulators[:, 2]
    shift_two = modulators[:, 3]
    scale_two = modulators[:, 4]
    gate_two = modulators[:, 5]
    residual = swapped.astype(jnp.float32)
    normed_full, modulate_back_one = jax.vjp(modulate, residual, shift_one, scale_one)
    normed_one = normed_full.astype(jnp.bfloat16).reshape(row_count, model_width)
    bias_full = jnp.concatenate(
        [qv_bias[:model_width], jnp.zeros((model_width,), jnp.bfloat16), qv_bias[model_width:]]
    ).astype(jnp.float32)
    projected = (
        jnp.dot(normed_one, qkv_weight, preferred_element_type=jnp.float32) + bias_full
    ).astype(jnp.bfloat16)
    shaped = projected.reshape(clip_count, frames, patches, 3, HEADS, head_width)
    queries = shaped[:, :, :, 0]
    keys_all = shaped[:, :, :, 1]
    values_all = shaped[:, :, :, 2]
    scores = (
        jnp.einsum("cfphd,cgphd->cphfg", queries, keys_all, preferred_element_type=jnp.float32)
        * factor
    )
    scores = jnp.where(key_valid, scores, NEGATIVE)
    row_peak = jnp.max(scores, axis=-1, keepdims=True)
    exponent = jnp.exp(scores - row_peak)
    attention_weights = exponent / jnp.sum(exponent, axis=-1, keepdims=True)
    weights_low = attention_weights.astype(jnp.bfloat16)
    context = jnp.einsum(
        "cphfg,cgphd->cfphd", weights_low, values_all, preferred_element_type=jnp.float32
    )
    context_low = context.astype(jnp.bfloat16).reshape(row_count, model_width)
    attended = jnp.dot(
        context_low, out_weight, preferred_element_type=jnp.float32
    ) + out_bias.astype(jnp.float32)
    attended = attended.reshape(clip_count, frames, patches, model_width)
    middle = residual + gate_one * attended
    normed_mid, modulate_back_two = jax.vjp(modulate, middle, shift_two, scale_two)
    normed_two = normed_mid.astype(jnp.bfloat16).reshape(row_count, model_width)
    hidden = jnp.dot(normed_two, fc1_weight, preferred_element_type=jnp.float32) + fc1_bias.astype(
        jnp.float32
    )
    activated_full, gelu_back = jax.vjp(gelu_tanh, hidden)
    activated = activated_full.astype(jnp.bfloat16)
    branch_two = jnp.dot(
        activated, fc2_weight, preferred_element_type=jnp.float32
    ) + fc2_bias.astype(jnp.float32)
    branch_two = branch_two.reshape(clip_count, frames, patches, model_width)
    result = valid_rows * (middle + gate_two * branch_two)
    block_output = lax.all_to_all(
        result.astype(jnp.bfloat16), "frame", split_axis=1, concat_axis=2, tiled=True
    )
    cotangent = lax.all_to_all(
        out_cotangent, "frame", split_axis=2, concat_axis=1, tiled=True
    ).astype(jnp.float32)
    d_result = valid_rows * cotangent
    d_gate_two = jnp.sum(d_result * branch_two, axis=(1, 2))
    d_branch = (d_result * gate_two).astype(jnp.bfloat16).reshape(row_count, model_width)
    d_fc2_bias = jnp.sum(d_branch.astype(jnp.float32), axis=0)
    d_fc2_weight = contract_rows(activated, d_branch)
    d_activated = contract_cols(d_branch, fc2_weight)
    d_hidden = gelu_back(d_activated)[0].astype(jnp.bfloat16)
    d_fc1_bias = jnp.sum(d_hidden.astype(jnp.float32), axis=0)
    d_fc1_weight = contract_rows(normed_two, d_hidden)
    d_normed_two = contract_cols(d_hidden, fc1_weight).reshape(
        clip_count, frames, patches, model_width
    )
    d_middle_norm, d_shift_two, d_scale_two = modulate_back_two(d_normed_two)
    d_middle = d_result + d_middle_norm
    d_gate_one = jnp.sum(d_middle * attended, axis=(1, 2))
    d_attended = (d_middle * gate_one).astype(jnp.bfloat16).reshape(row_count, model_width)
    d_out_bias = jnp.sum(d_attended.astype(jnp.float32), axis=0)
    d_out_weight = contract_rows(context_low, d_attended)
    d_context = contract_cols(d_attended, out_weight).astype(jnp.bfloat16)
    d_context = d_context.reshape(clip_count, frames, patches, HEADS, head_width)
    d_weights = jnp.einsum(
        "cfphd,cgphd->cphfg", d_context, values_all, preferred_element_type=jnp.float32
    )
    d_values = jnp.einsum(
        "cphfg,cfphd->cgphd", weights_low, d_context, preferred_element_type=jnp.float32
    )
    d_scores = attention_weights * (
        d_weights - jnp.sum(attention_weights * d_weights, axis=-1, keepdims=True)
    )
    d_scores = d_scores.astype(jnp.bfloat16)
    d_queries = (
        jnp.einsum("cphfg,cgphd->cfphd", d_scores, keys_all, preferred_element_type=jnp.float32)
        * factor
    )
    d_keys = (
        jnp.einsum("cphfg,cfphd->cgphd", d_scores, queries, preferred_element_type=jnp.float32)
        * factor
    )
    d_projected = (
        jnp.stack([d_queries, d_keys, d_values], axis=3)
        .astype(jnp.bfloat16)
        .reshape(row_count, 3 * model_width)
    )
    column_sums = jnp.sum(d_projected.astype(jnp.float32), axis=0)
    d_qv_bias = jnp.concatenate([column_sums[:model_width], column_sums[2 * model_width :]])
    d_qkv_weight = contract_rows(normed_one, d_projected)
    d_normed_one = contract_cols(d_projected, qkv_weight).reshape(
        clip_count, frames, patches, model_width
    )
    d_residual, d_shift_one, d_scale_one = modulate_back_one(d_normed_one)
    d_input = d_middle + d_residual
    input_grad = lax.all_to_all(
        d_input.astype(jnp.bfloat16), "frame", split_axis=1, concat_axis=2, tiled=True
    )
    d_modulation = jnp.stack(
        [
            d_shift_one.reshape(clip_count, model_width),
            d_scale_one.reshape(clip_count, model_width),
            d_gate_one,
            d_shift_two.reshape(clip_count, model_width),
            d_scale_two.reshape(clip_count, model_width),
            d_gate_two,
        ],
        axis=1,
    ).reshape(clip_count, 6 * model_width)
    every_part = (
        lax.psum_scatter(d_qkv_weight, "frame", scatter_dimension=1, tiled=True),
        lax.psum_scatter(d_out_weight, "frame", scatter_dimension=1, tiled=True),
        lax.psum_scatter(d_fc1_weight, "frame", scatter_dimension=1, tiled=True),
        lax.psum_scatter(d_fc2_weight, "frame", scatter_dimension=1, tiled=True),
        lax.psum_scatter(d_modulation, "frame", scatter_dimension=1, tiled=True),
        lax.psum_scatter(d_qv_bias, "frame", scatter_dimension=0, tiled=True),
        lax.psum_scatter(d_out_bias, "frame", scatter_dimension=0, tiled=True),
        lax.psum_scatter(d_fc1_bias, "frame", scatter_dimension=0, tiled=True),
        lax.psum_scatter(d_fc2_bias, "frame", scatter_dimension=0, tiled=True),
    )
    every_mat = (
        lax.psum_scatter(every_part[0], "clip", scatter_dimension=0, tiled=True),
        lax.psum_scatter(every_part[1], "clip", scatter_dimension=0, tiled=True),
        lax.psum_scatter(every_part[2], "clip", scatter_dimension=0, tiled=True),
        lax.psum_scatter(every_part[3], "clip", scatter_dimension=0, tiled=True),
    )
    qkv_grad = every_mat[0]
    out_grad = every_mat[1]
    fc1_grad = every_mat[2]
    fc2_grad = every_mat[3]
    modulation_grad = every_part[4]
    bias_parts = (every_part[5], every_part[6], every_part[7], every_part[8])
    bias_totals = lax.psum((bias_parts[0], bias_parts[1], bias_parts[2], bias_parts[3]), "clip")
    return (
        block_output,
        input_grad,
        modulation_grad,
        qkv_grad,
        bias_totals[0],
        out_grad,
        bias_totals[1],
        fc1_grad,
        bias_totals[2],
        fc2_grad,
        bias_totals[3],
    )


def solution(mesh):
    placed = (
        P("clip", "frame", None, None),
        P("clip", None),
        P("clip"),
        P(),
        P(),
        P(),
        P(),
        P(),
        P(),
        P(),
        P(),
        P("clip", "frame", None, None),
    )
    return jax.shard_map(
        on_device,
        mesh=mesh,
        in_specs=placed,
        out_specs=(
            P("clip", "frame", None, None),
            P("clip", "frame", None, None),
            P("clip", "frame"),
            P("clip", "frame"),
            P("frame"),
            P("clip", "frame"),
            P("frame"),
            P("clip", "frame"),
            P("frame"),
            P("clip", "frame"),
            P("frame"),
        ),
        check_vma=False,
    )
```

profile of v0, /device:TPU:0, one launch (start us, length us, event | category | flops | bytes accessed | tf_op | source)
XLA Modules:
  0.0 1028.3 jit_solution(13910262976260021615)
XLA Ops:
  19.6 12.0 %all-to-all-done = bf16[2,4,64,1152]{3,1,0,2:T(4,128)(2,1)} async-done(((bf16[2,4,64,1152]{3,1,0,2:T(4,128)(2,1)}), bf16[2,4,64,1152]{3,1,0,2:T(4,128)(2,1)}, u32[]{:S(2)}, u32[]{:S(2)}) %all-to-all-start) | async-done | bytes 1179680 | tf_op jit(solution)/shard_map/all_to_all | solution.py:51
  43.7 10.0 add_convert_fusion
  53.8 13.6 %reshape.417 = bf16[2,16,16,3,16,72]{5,4,3,2,1,0:T(8,128)(2,1)} reshape(bf16[512,3456]{1,0:T(8,128)(2,1)} %add_convert_fusion) | data formatting | bytes 7077888 | tf_op jit(solution)/shard_map/reshape | solution.py:77
  98.9 9.5 fusion.53
  113.1 10.3 %fusion.42 = f32[4608,1152]{0,1:T(8,128)} fusion(bf16[512,1152]{1,0:T(8,128)(2,1)S(1)} %fusion.19, f32[512,4608]{1,0:T(8,128)S(1)} %fusion.53, f32[4608]{0:T(1024)S(1)} %convert_element_type.207), kind=kOutput, calls=%fused_computation.115 | convolution fusion | flops 5459410944 | bytes 31868928 | tf_op jit(solution)/shard_map/dot_general | solution.py:26
  124.1 15.8 %convert_reduce_fusion.1 = (f32[4608]{0:T(1024)S(1)}, bf16[512,4608]{1,0:T(8,128)(2,1)S(1)}) fusion(f32[512,4608]{1,0:T(8,128)} %copy-done.47, f32[4608]{0:T(1024)S(1)} %convert_element_type.207, bf16[512,1152]{1,0:T(8,128)(2,1)} %copy-done.33, bf16[4608,1152]{1,0:T(8,128)(2,1)} %param.21), kind=kOutput, calls=%fused_computation.12 | convolution fusion | flops 5490077184 | bytes 25989120 | tf_op jit(solution)/shard_map/dot_general | solution.py:32
  139.9 11.1 %fusion.54 = f32[512,1152]{1,0:T(8,128)S(1)} fusion(bf16[512,4608]{1,0:T(8,128)(2,1)S(1)} %get-tuple-element.58, bf16[1152,4608]{1,0:T(8,128)(2,1)} %param.19), kind=kOutput, calls=%fused_computation.126 | convolution fusion | flops 5435817984 | bytes 17694720 | tf_op jit(solution)/shard_map/dot_general | solution.py:32
  193.0 11.3 %convert_element_type.223 = bf16[2,16,16,3456]{3,2,1,0:T(8,128)(2,1)} reshape(bf16[2,16,16,3,16,72]{5,4,3,2,1,0:T(8,128)(2,1)} %copy.71) | data formatting | bytes 7077888 | tf_op jit(solution)/shard_map/convert_element_type | solution.py:157
  204.3 11.0 %convert_element_type.227 = bf16[512,3456]{1,0:T(8,128)(2,1)} reshape(bf16[2,16,16,3,16,72]{5,4,3,2,1,0:T(8,128)(2,1)} %copy.71) | data formatting | bytes 7077888 | tf_op jit(solution)/shard_map/convert_element_type | solution.py:157
  215.3 9.8 multiply_reduce_fusion.4
  227.2 13.6 %convolution_add_fusion = f32[512,1152]{1,0:T(8,128)S(1)} fusion(bf16[4608,1152]{1,0:T(8,128)(2,1)} %param.21, f32[1152]{0:T(1024)S(1)} %convert_element_type.209, f32[512,4608]{1,0:T(8,128)} %copy-done.47, f32[4608]{0:T(1024)S(1)} %convert_element_type.207), kind=kOutput, calls=%fused_computation.30 | convolution fusion | flops 5460000768 | bytes 22436352 | tf_op jit(solution)/shard_map/dot_general | solution.py:106
  245.8 8.4 fusion.55
  255.8 12.2 %fusion.57 = f32[1152,4608]{1,0:T(8,128)} fusion(bf16[512,1152]{1,0:T(8,128)(2,1)S(1)} %copy-done.23, bf16[512,4608]{1,0:T(8,128)(2,1)} %copy-done.21), kind=kOutput, calls=%fused_computation.129 | convolution fusion | flops 5435817984 | bytes 27131904 | tf_op jit(solution)/shard_map/dot_general | solution.py:26
  271.0 44.4 %reduce-scatter.26.cloned.1.call-done = f32[4608,288]{0,1:T(8,128)} async-done(((f32[4608,1152]{0,1:T(8,128)}), f32[4608,288]{0,1:T(8,128)}) %reduce-scatter.26.cloned.1.call-update) | async-done | bytes 5308432 | tf_op jit(solution)/shard_map/reduce_scatter | solution.py:186
  322.2 58.5 %reduce-scatter.20.cloned.1.call-done = f32[1152,288]{0,1:T(8,128)} async-done(((f32[1152,1152]{0,1:T(8,128)}), f32[1152,288]{0,1:T(8,128)}) %reduce-scatter.20.cloned.1.call-update) | async-done | bytes 1327120 | tf_op jit(solution)/shard_map/reduce_scatter | solution.py:184
  383.9 147.6 %reduce-scatter.18.cloned.1.call-done = f32[1152,864]{0,1:T(8,128)} async-done(((f32[1152,3456]{0,1:T(8,128)}), f32[1152,864]{0,1:T(8,128)}) %reduce-scatter.18.cloned.1.call-update) | async-done | bytes 3981328 | tf_op jit(solution)/shard_map/reduce_scatter | solution.py:183
  537.1 187.3 %reduce-scatter.22.cloned.1.call-done = f32[1152,1152]{1,0:T(8,128)} async-done(((f32[1152,4608]{1,0:T(8,128)}), f32[1152,1152]{1,0:T(8,128)}) %reduce-scatter.22.cloned.1.call-update) | async-done | bytes 5308432 | tf_op jit(solution)/shard_map/reduce_scatter | solution.py:185
  734.2 21.7 %all-to-all-done.3 = bf16[2,16,16,1152]{3,2,0,1:T(8,128)(2,1)S(1)} async-done(((bf16[2,16,16,1152]{3,2,0,1:T(8,128)(2,1)}), bf16[2,16,16,1152]{3,2,0,1:T(8,128)(2,1)S(1)}, u32[]{:S(2)}, u32[]{:S(2)}) %all-to-all-start.3) | async-done | bytes 1179680 | tf_op jit(solution)/shard_map/all_to_all | solution.py:168
  762.4 25.4 %all-reduce.5 = (f32[2304]{0:T(1024)S(1)}, f32[1152]{0:T(1024)S(1)}, f32[4608]{0:T(1024)S(1)}, f32[1152]{0:T(1024)S(1)}) all-reduce(f32[2304]{0:T(1024)S(1)} %pad_maximum_fusion, f32[1152]{0:T(1024)S(1)} %get-tuple-element.59, f32[4608]{0:T(1024)S(1)} %get-tuple-element.57, ...), channel_id=5, replica_groups=mesh['clip'=8,'frame'=4] {'frame'}, use_global_device_ids=true, to_apply=%region_21.22.clone | all-reduce | flops 9216 | bytes 73728
  788.2 26.7 %all-reduce.4 = (f32[576]{0:T(1024)}, f32[288]{0:T(512)}, f32[1152]{0:T(1024)}, f32[288]{0:T(512)}) all-reduce(f32[576]{0:T(1024)S(1)} %dynamic-slice.1, f32[288]{0:T(512)S(1)} %dynamic-slice.3, f32[1152]{0:T(1024)S(1)} %dynamic-slice.5, f32[288]{0:T(512)S(1)} %dynamic-slice.7), channel_id=1, replica_groups=mesh['clip'=8,'frame'=4] {'clip'}, use_global_device_ids=true, to_apply=%region_22.23 | all-reduce | flops 2304 | bytes 18432 | tf_op jit(solution)/shard_map/psum | solution.py:205
  821.9 51.5 %reduce-scatter.34.cloned.1.call-done = f32[576,288]{1,0:T(8,128)} async-done(((f32[4608,288]{1,0:T(8,128)}), f32[576,288]{1,0:T(8,128)}) %reduce-scatter.34.cloned.1.call-update) | async-done | bytes 663568
  875.7 33.6 %reduce-scatter.32.cloned.1.call-done = f32[144,288]{1,0:T(8,128)} async-done(((f32[1152,288]{1,0:T(8,128)}), f32[144,288]{1,0:T(8,128)}) %reduce-scatter.32.cloned.1.call-update) | async-done | bytes 165904
  909.3 50.7 %reduce-scatter.30.cloned.1.call-done = f32[144,864]{1,0:T(8,128)} async-done(((f32[1152,864]{1,0:T(8,128)}), f32[144,864]{1,0:T(8,128)}) %reduce-scatter.30.cloned.1.call-update) | async-done | bytes 497680
  960.0 61.6 %reduce-scatter.24.cloned.1.call-done = f32[144,1152]{1,0:T(8,128)} async-done(((f32[1152,1152]{1,0:T(8,128)}), f32[144,1152]{1,0:T(8,128)}) %reduce-scatter.24.cloned.1.call-update) | async-done | bytes 663568 | tf_op jit(solution)/shard_map/reduce_scatter | solution.py:196
  (217 shorter events, 153.8 us)
Async XLA Ops:
  7.2 79.0 %copy-start = (bf16[1152,1152]{1,0:T(8,128)(2,1)S(1)}, bf16[1152,1152]{1,0:T(8,128)(2,1)}, u32[]{:S(2)}) copy-start(bf16[1152,1152]{1,0:T(8,128)(2,1)} %param.17) | copy-start | bytes 7962628
  10.6 21.0 %all-to-all-start = ((bf16[2,4,64,1152]{3,1,0,2:T(4,128)(2,1)}), bf16[2,4,64,1152]{3,1,0,2:T(4,128)(2,1)}, u32[]{:S(2)}, u32[]{:S(2)}) async-start(bf16[2,4,64,1152]{3,1,0,2:T(4,128)(2,1)} %copy.57), calls=%async_computation | async-start | bytes 2359296 | tf_op jit(solution)/shard_map/all_to_all | solution.py:51
  16.1 15.5 %copy-start.40 = (f32[2,16]{1,0:T(2,128)}, f32[2,16]{1,0:T(2,128)S(1)}, u32[]{:S(2)}) copy-start(f32[2,16]{1,0:T(2,128)S(1)} %get-tuple-element.97) | copy-start | bytes 388
  19.5 22.2 %copy-start.34 = (f32[2,1152]{1,0:T(2,128)}, f32[2,1152]{1,0:T(2,128)S(1)}, u32[]{:S(2)}) copy-start(f32[2,1152]{1,0:T(2,128)S(1)} %get-tuple-element.106) | copy-start | bytes 27652
  31.6 62.3 %all-to-all-start.2 = ((bf16[2,4,64,1152]{3,1,0,2:T(4,128)(2,1)}), bf16[2,4,64,1152]{3,1,0,2:T(4,128)(2,1)}, u32[]{:S(2)}, u32[]{:S(2)}) async-start(bf16[2,4,64,1152]{3,1,0,2:T(4,128)(2,1)} %copy.66), calls=%async_computation.2 | async-start | bytes 2359296 | tf_op jit(solution)/shard_map/all_to_all | solution.py:114
  35.9 279.5 %reduce-scatter.26.cloned.1.call-start = ((), (), s32[]{:S(2)}) async-start(), calls=%async_computation.17 | async-start | bytes 26542080 | tf_op jit(solution)/shard_map/reduce_scatter | solution.py:186
  95.6 12.9 %copy-start.9 = (f32[2,4,4,16,1152]{4,3,1,2,0:T(8,128)}, f32[2,4,4,16,1152]{4,3,1,2,0:T(8,128)S(1)}, u32[]{:S(2)}) copy-start(f32[2,4,4,16,1152]{4,3,1,2,0:T(8,128)S(1)} %copy.67) | copy-start | bytes 7077892
  123.5 257.3 %reduce-scatter.20.cloned.1.call-start = ((), (), s32[]{:S(2)}) async-start(), calls=%async_computation.14 | async-start | bytes 6635520 | tf_op jit(solution)/shard_map/reduce_scatter | solution.py:184
  139.9 11.1 %copy-start.21 = (bf16[512,4608]{1,0:T(8,128)(2,1)}, bf16[512,4608]{1,0:T(8,128)(2,1)S(1)}, u32[]{:S(2)}) copy-start(bf16[512,4608]{1,0:T(8,128)(2,1)S(1)} %get-tuple-element.58) | copy-start | bytes 14155780
  139.9 12.5 %copy-start.14 = (f32[2,4,4,16,1152]{4,3,2,1,0:T(8,128)S(1)}, f32[2,4,4,16,1152]{4,3,2,1,0:T(8,128)}, u32[]{:S(2)}) copy-start(f32[2,4,4,16,1152]{4,3,2,1,0:T(8,128)} %get-tuple-element.69) | copy-start | bytes 7077892
  163.0 368.5 %reduce-scatter.18.cloned.1.call-start = ((), (), s32[]{:S(2)}) async-start(), calls=%async_computation.13 | async-start | bytes 19906560 | tf_op jit(solution)/shard_map/reduce_scatter | solution.py:183
  204.3 11.0 %copy-start.4 = (f32[2,4,4,16,1152]{4,3,1,2,0:T(8,128)S(1)}, f32[2,4,4,16,1152]{4,3,1,2,0:T(8,128)}, u32[]{:S(2)}) copy-start(f32[2,4,4,16,1152]{4,3,1,2,0:T(8,128)} %copy-done.2) | copy-start | bytes 7077892
  215.3 9.9 copy-start.13
  227.2 13.7 %copy-start.11 = (f32[2,4,4,16,1152]{4,3,1,2,0:T(8,128)S(1)}, f32[2,4,4,16,1152]{4,3,1,2,0:T(8,128)}, u32[]{:S(2)}) copy-start(f32[2,4,4,16,1152]{4,3,1,2,0:T(8,128)} %copy-done.9) | copy-start | bytes 7077892
  227.2 13.7 %copy-start.41 = (f32[2,16]{1,0:T(2,128)S(1)}, f32[2,16]{1,0:T(2,128)}, u32[]{:S(2)}) copy-start(f32[2,16]{1,0:T(2,128)} %copy-done.40) | copy-start | bytes 388
  254.2 470.2 %reduce-scatter.22.cloned.1.call-start = ((), (), s32[]{:S(2)}) async-start(), calls=%async_computation.15 | async-start | bytes 26542080 | tf_op jit(solution)/shard_map/reduce_scatter | solution.py:185
  268.0 546.8 %reduce-scatter.28.cloned.1.call-start = ((), (), s32[]{:S(2)}) async-start(), calls=%async_computation.18 | async-start | bytes 4423680
  271.0 602.4 %reduce-scatter.34.cloned.1.call-start = ((), (), s32[]{:S(2)}) async-start(), calls=%async_computation.21 | async-start | bytes 7962624
  322.1 587.2 %reduce-scatter.32.cloned.1.call-start = ((), (), s32[]{:S(2)}) async-start(), calls=%async_computation.20 | async-start | bytes 1990656
  383.8 576.1 %reduce-scatter.30.cloned.1.call-start = ((), (), s32[]{:S(2)}) async-start(), calls=%async_computation.19 | async-start | bytes 4644864
  537.0 484.5 %reduce-scatter.24.cloned.1.call-start = ((), (), s32[]{:S(2)}) async-start(), calls=%async_computation.16 | async-start | bytes 5971968 | tf_op jit(solution)/shard_map/reduce_scatter | solution.py:196
  726.8 29.1 %all-to-all-start.3 = ((bf16[2,16,16,1152]{3,2,0,1:T(8,128)(2,1)}), bf16[2,16,16,1152]{3,2,0,1:T(8,128)(2,1)S(1)}, u32[]{:S(2)}, u32[]{:S(2)}) async-start(bf16[2,16,16,1152]{3,2,0,1:T(8,128)(2,1)} %copy.72), calls=%async_computation.3 | async-start | bytes 2359296 | tf_op jit(solution)/shard_map/all_to_all | solution.py:168
  755.9 63.6 %all-to-all-start.1 = ((bf16[2,16,16,1152]{3,2,0,1:T(8,128)(2,1)}), bf16[2,16,16,1152]{3,2,0,1:T(8,128)(2,1)}, u32[]{:S(2)}, u32[]{:S(2)}) async-start(bf16[2,16,16,1152]{3,2,0,1:T(8,128)(2,1)} %copy.64), calls=%async_computation.1 | async-start | bytes 2359296 | tf_op jit(solution)/shard_map/all_to_all | solution.py:111
  816.9 204.6 %copy-start.1 = (bf16[1152,1152]{1,0:T(8,128)(2,1)S(1)}, bf16[1152,1152]{1,0:T(8,128)(2,1)}, u32[]{:S(2)}) copy-start(bf16[1152,1152]{1,0:T(8,128)(2,1)} %param.17) | copy-start | bytes 7962628
  (37 other events, 160.3 us)
Sparse Core Ops, SparseCore 0:
  123.6 191.7 reduce-scatter.25
  318.7 61.9 reduce-scatter.19
  384.1 147.2 reduce-scatter.17
  534.4 189.9 reduce-scatter.21
  727.6 65.9 reduce-scatter.27
  795.9 77.4 reduce-scatter.33
  876.3 32.9 reduce-scatter.31
  912.3 47.6 reduce-scatter.29
  962.9 58.6 reduce-scatter.23
where the time goes:
time: 1030 us
  waiting for transfers between devices  669 us (65%)
  matrix products  129 us (13%)
  local copies, waits for them, and re-layouts  112 us (11%)
  blocking collectives  52.1 us (5%)
  other arithmetic  31.5 us (3%)
  starting transfers between devices  17.8 us (2%)
  between operations  16.9 us (2%)
    reduce_scatter x1, waiting for transfers between devices, on_device(): lax.psum_scatter(d_fc1_weight, 'frame', scatter_dimension=1, tiled=True)  187 us
    reduce_scatter x1, waiting for transfers between devices, on_device(): lax.psum_scatter(d_qkv_weight, 'frame', scatter_dimension=1, tiled=True)  148 us
    unnamed x13, waiting for transfers between devices  136 us
    reduce_scatter x1, waiting for transfers between devices, on_device(): lax.psum_scatter(every_part[2], 'clip', scatter_dimension=0, tiled=True)  61.6 us
    reduce_scatter x1, waiting for transfers between devices, on_device(): lax.psum_scatter(d_out_weight, 'frame', scatter_dimension=1, tiled=True)  58.5 us
    reduce_scatter x1, waiting for transfers between devices, on_device(): lax.psum_scatter(d_fc2_weight, 'frame', scatter_dimension=1, tiled=True)  44.4 us
    unnamed x113, local copies, waits for them, and re-layouts  43.8 us
    dot_general x4, matrix products, contract_cols(): lax.dot_general(left, right, (((1,), (1,)), ((), ())), preferred_element_...  40.8 us
  transfers between devices with their start and end apart: 13, of which 10 were waited for; matrix products, arithmetic and copies ran while one was open for 22% of the time, Pallas kernels for 0%

commit v1 on v0

--- a/solution.py
+++ b/solution.py
@@ -165,9 +165,20 @@
     )
     d_residual, d_shift_one, d_scale_one = modulate_back_one(d_normed_one)
     d_input = d_middle + d_residual
-    input_grad = lax.all_to_all(
-        d_input.astype(jnp.bfloat16), "frame", split_axis=1, concat_axis=2, tiled=True
-    )
+    x = d_input.astype(jnp.bfloat16)
+    ways, here = (lax.axis_size("frame"), lax.axis_index("frame"))
+    width = x.shape[1] // ways
+    dims = list(x.shape)
+    dims[1] = width
+    height = dims[2]
+    dims[2] = height * ways
+    full = jnp.zeros(dims, x.dtype)
+    for mask in range(ways):
+        part = lax.dynamic_slice_in_dim(x, (here ^ mask) * width, width, axis=1)
+        if mask:
+            part = lax.ppermute(part, "frame", [(d, d ^ mask) for d in range(ways)])
+        full = lax.dynamic_update_slice_in_dim(full, part, (here ^ mask) * height, axis=2)
+    input_grad = full
     d_modulation = jnp.stack(
         [
             d_shift_one.reshape(clip_count, model_width),

time: 1030 us -> 1030 us (level)
  waiting for transfers between devices: 669 us -> 654 us
  blocking collectives: 52.1 us -> 65.4 us
    all_to_all x1 -> x0, waiting for transfers between devices: 21.7 us -> none  [on_device(): lax.all_to_all(d_input.astype(jnp.bfloat16), 'frame', split_axis=1, conca...]
    unnamed x1, blocking collectives: 25.4 us -> 38.9 us
    unnamed x113 -> x115, local copies, waits for them, and re-layouts: 43.8 us -> 43.9 us
  transfers between devices with their start and end apart: 13 -> 15, of which waited for: 10 -> 9; matrix products, arithmetic and copies ran while one was open for 22% -> 23% of each run, Pallas kernels for 0% -> 0%
where the time goes in v1:
time: 1030 us
  waiting for transfers between devices  654 us (63%)
  matrix products  129 us (13%)
  local copies, waits for them, and re-layouts  113 us (11%)
  blocking collectives  65.4 us (6%)
  other arithmetic  33 us (3%)
  between operations  16.9 us (2%)
  starting transfers between devices  16.3 us (2%)
    reduce_scatter x1, waiting for transfers between devices, on_device(): lax.psum_scatter(d_fc1_weight, 'frame', scatter_dimension=1, tiled=True)  187 us
    reduce_scatter x1, waiting for transfers between devices, on_device(): lax.psum_scatter(d_qkv_weight, 'frame', scatter_dimension=1, tiled=True)  148 us
    unnamed x13, waiting for transfers between devices  144 us
    reduce_scatter x1, waiting for transfers between devices, on_device(): lax.psum_scatter(every_part[2], 'clip', scatter_dimension=0, tiled=True)  61.6 us
    reduce_scatter x1, waiting for transfers between devices, on_device(): lax.psum_scatter(d_out_weight, 'frame', scatter_dimension=1, tiled=True)  58.5 us
    unnamed x115, local copies, waits for them, and re-layouts  43.9 us
    reduce_scatter x1, waiting for transfers between devices, on_device(): lax.psum_scatter(d_fc2_weight, 'frame', scatter_dimension=1, tiled=True)  43.2 us
    dot_general x4, matrix products, contract_cols(): lax.dot_general(left, right, (((1,), (1,)), ((), ())), preferred_element_...  41.5 us
  transfers between devices with their start and end apart: 15, of which 9 were waited for; matrix products, arithmetic and copies ran while one was open for 23% of the time, Pallas kernels for 0%

profile of v1, /device:TPU:0, one launch (start us, length us, event | category | flops | bytes accessed | tf_op | source)
XLA Modules:
  0.0 1028.5 jit_solution(10134538719304925673)
XLA Ops:
  19.6 12.0 %all-to-all-done = bf16[2,4,64,1152]{3,1,0,2:T(4,128)(2,1)} async-done(((bf16[2,4,64,1152]{3,1,0,2:T(4,128)(2,1)}), bf16[2,4,64,1152]{3,1,0,2:T(4,128)(2,1)}, u32[]{:S(2)}, u32[]{:S(2)}) %all-to-all-start) | async-done | bytes 1179680 | tf_op jit(solution)/shard_map/all_to_all | solution.py:51
  43.7 10.0 add_convert_fusion
  53.7 13.6 %reshape.417 = bf16[2,16,16,3,16,72]{5,4,3,2,1,0:T(8,128)(2,1)} reshape(bf16[512,3456]{1,0:T(8,128)(2,1)} %add_convert_fusion) | data formatting | bytes 7077888 | tf_op jit(solution)/shard_map/reshape | solution.py:77
  98.8 9.5 fusion.53
  113.0 10.4 %fusion.42 = f32[4608,1152]{0,1:T(8,128)} fusion(bf16[512,1152]{1,0:T(8,128)(2,1)S(1)} %fusion.19, f32[512,4608]{1,0:T(8,128)S(1)} %fusion.53, f32[4608]{0:T(1024)S(1)} %convert_element_type.207), kind=kOutput, calls=%fused_computation.122 | convolution fusion | flops 5459410944 | bytes 31868928 | tf_op jit(solution)/shard_map/dot_general | solution.py:26
  124.1 16.4 %convert_reduce_fusion.1 = (f32[4608]{0:T(1024)}, bf16[512,4608]{1,0:T(8,128)(2,1)S(1)}) fusion(f32[512,4608]{1,0:T(8,128)} %copy-done.48, f32[4608]{0:T(1024)S(1)} %convert_element_type.207, bf16[512,1152]{1,0:T(8,128)(2,1)} %copy-done.32, bf16[4608,1152]{1,0:T(8,128)(2,1)} %param.21), kind=kOutput, calls=%fused_computation.12 | convolution fusion | flops 5490077184 | bytes 25989120 | tf_op jit(solution)/shard_map/dot_general | solution.py:32
  140.5 10.9 %fusion.54 = f32[512,1152]{1,0:T(8,128)S(1)} fusion(bf16[512,4608]{1,0:T(8,128)(2,1)S(1)} %get-tuple-element.58, bf16[1152,4608]{1,0:T(8,128)(2,1)} %param.19), kind=kOutput, calls=%fused_computation.133 | convolution fusion | flops 5435817984 | bytes 17694720 | tf_op jit(solution)/shard_map/dot_general | solution.py:32
  173.5 7.0 multiply_reduce_fusion
  194.3 11.3 %convert_element_type.223 = bf16[2,16,16,3456]{3,2,1,0:T(8,128)(2,1)} reshape(bf16[2,16,16,3,16,72]{5,4,3,2,1,0:T(8,128)(2,1)} %copy.69) | data formatting | bytes 7077888 | tf_op jit(solution)/shard_map/convert_element_type | solution.py:157
  205.6 11.0 %convert_element_type.227 = bf16[512,3456]{1,0:T(8,128)(2,1)} reshape(bf16[2,16,16,3,16,72]{5,4,3,2,1,0:T(8,128)(2,1)} %copy.69) | data formatting | bytes 7077888 | tf_op jit(solution)/shard_map/convert_element_type | solution.py:157
  216.7 9.9 multiply_reduce_fusion.4
  228.6 13.3 %convolution_add_fusion = f32[512,1152]{1,0:T(8,128)S(1)} fusion(bf16[4608,1152]{1,0:T(8,128)(2,1)} %param.21, f32[1152]{0:T(1024)S(1)} %convert_element_type.209, f32[512,4608]{1,0:T(8,128)} %copy-done.48, f32[4608]{0:T(1024)S(1)} %convert_element_type.207), kind=kOutput, calls=%fused_computation.30 | convolution fusion | flops 5460000768 | bytes 22436352 | tf_op jit(solution)/shard_map/dot_general | solution.py:106
  247.1 8.7 fusion.55
  257.1 12.2 %fusion.57 = f32[1152,4608]{1,0:T(8,128)} fusion(bf16[512,1152]{1,0:T(8,128)(2,1)S(1)} %copy-done.23, bf16[512,4608]{1,0:T(8,128)(2,1)} %copy-done.21), kind=kOutput, calls=%fused_computation.136 | convolution fusion | flops 5435817984 | bytes 27131904 | tf_op jit(solution)/shard_map/dot_general | solution.py:26
  272.3 43.2 %reduce-scatter.26.cloned.1.call-done = f32[4608,288]{0,1:T(8,128)} async-done(((f32[4608,1152]{0,1:T(8,128)}), f32[4608,288]{0,1:T(8,128)}) %reduce-scatter.26.cloned.1.call-update) | async-done | bytes 5308432 | tf_op jit(solution)/shard_map/reduce_scatter | solution.py:197
  322.2 58.5 %reduce-scatter.20.cloned.1.call-done = f32[1152,288]{0,1:T(8,128)} async-done(((f32[1152,1152]{0,1:T(8,128)}), f32[1152,288]{0,1:T(8,128)}) %reduce-scatter.20.cloned.1.call-update) | async-done | bytes 1327120 | tf_op jit(solution)/shard_map/reduce_scatter | solution.py:195
  383.9 147.5 %reduce-scatter.18.cloned.1.call-done = f32[1152,864]{0,1:T(8,128)} async-done(((f32[1152,3456]{0,1:T(8,128)}), f32[1152,864]{0,1:T(8,128)}) %reduce-scatter.18.cloned.1.call-update) | async-done | bytes 3981328 | tf_op jit(solution)/shard_map/reduce_scatter | solution.py:194
  537.1 187.3 %reduce-scatter.22.cloned.1.call-done = f32[1152,1152]{1,0:T(8,128)} async-done(((f32[1152,4608]{1,0:T(8,128)}), f32[1152,1152]{1,0:T(8,128)}) %reduce-scatter.22.cloned.1.call-update) | async-done | bytes 5308432 | tf_op jit(solution)/shard_map/reduce_scatter | solution.py:196
  739.4 38.9 %all-reduce.5 = (f32[2304]{0:T(1024)S(1)}, f32[1152]{0:T(1024)S(1)}, f32[4608]{0:T(1024)S(1)}, f32[1152]{0:T(1024)S(1)}) all-reduce(f32[2304]{0:T(1024)S(1)} %pad_maximum_fusion, f32[1152]{0:T(1024)} %get-tuple-element.59, f32[4608]{0:T(1024)} %get-tuple-element.57, ...), channel_id=5, replica_groups=mesh['clip'=8,'frame'=4] {'frame'}, use_global_device_ids=true, to_apply=%region_21.22.clone | all-reduce | flops 9216 | bytes 73728
  778.6 26.5 %all-reduce.4 = (f32[576]{0:T(1024)}, f32[288]{0:T(512)}, f32[1152]{0:T(1024)}, f32[288]{0:T(512)}) all-reduce(f32[576]{0:T(1024)S(1)} %dynamic-slice.1, f32[288]{0:T(512)S(1)} %dynamic-slice.3, f32[1152]{0:T(1024)S(1)} %dynamic-slice.5, f32[288]{0:T(512)S(1)} %dynamic-slice.7), channel_id=1, replica_groups=mesh['clip'=8,'frame'=4] {'clip'}, use_global_device_ids=true, to_apply=%region_22.23 | all-reduce | flops 2304 | bytes 18432 | tf_op jit(solution)/shard_map/psum | solution.py:216
  813.9 59.5 %reduce-scatter.34.cloned.1.call-done = f32[576,288]{1,0:T(8,128)} async-done(((f32[4608,288]{1,0:T(8,128)}), f32[576,288]{1,0:T(8,128)}) %reduce-scatter.34.cloned.1.call-update) | async-done | bytes 663568
  875.7 33.8 %reduce-scatter.32.cloned.1.call-done = f32[144,288]{1,0:T(8,128)} async-done(((f32[1152,288]{1,0:T(8,128)}), f32[144,288]{1,0:T(8,128)}) %reduce-scatter.32.cloned.1.call-update) | async-done | bytes 165904
  909.5 50.7 %reduce-scatter.30.cloned.1.call-done = f32[144,864]{1,0:T(8,128)} async-done(((f32[1152,864]{1,0:T(8,128)}), f32[144,864]{1,0:T(8,128)}) %reduce-scatter.30.cloned.1.call-update) | async-done | bytes 497680
  960.2 61.6 %reduce-scatter.24.cloned.1.call-done = f32[144,1152]{1,0:T(8,128)} async-done(((f32[1152,1152]{1,0:T(8,128)}), f32[144,1152]{1,0:T(8,128)}) %reduce-scatter.24.cloned.1.call-update) | async-done | bytes 663568 | tf_op jit(solution)/shard_map/reduce_scatter | solution.py:207
  (226 shorter events, 147.9 us)
Async XLA Ops:
  7.2 79.0 %copy-start = (bf16[1152,1152]{1,0:T(8,128)(2,1)S(1)}, bf16[1152,1152]{1,0:T(8,128)(2,1)}, u32[]{:S(2)}) copy-start(bf16[1152,1152]{1,0:T(8,128)(2,1)} %param.17) | copy-start | bytes 7962628
  10.6 21.0 %all-to-all-start = ((bf16[2,4,64,1152]{3,1,0,2:T(4,128)(2,1)}), bf16[2,4,64,1152]{3,1,0,2:T(4,128)(2,1)}, u32[]{:S(2)}, u32[]{:S(2)}) async-start(bf16[2,4,64,1152]{3,1,0,2:T(4,128)(2,1)} %copy.55), calls=%async_computation | async-start | bytes 2359296 | tf_op jit(solution)/shard_map/all_to_all | solution.py:51
  16.1 15.5 %copy-start.41 = (f32[2,16]{1,0:T(2,128)}, f32[2,16]{1,0:T(2,128)S(1)}, u32[]{:S(2)}) copy-start(f32[2,16]{1,0:T(2,128)S(1)} %get-tuple-element.101) | copy-start | bytes 388
  19.5 22.1 %copy-start.34 = (f32[2,1152]{1,0:T(2,128)}, f32[2,1152]{1,0:T(2,128)S(1)}, u32[]{:S(2)}) copy-start(f32[2,1152]{1,0:T(2,128)S(1)} %get-tuple-element.110) | copy-start | bytes 27652
  31.6 62.3 %all-to-all-start.2 = ((bf16[2,4,64,1152]{3,1,0,2:T(4,128)(2,1)}), bf16[2,4,64,1152]{3,1,0,2:T(4,128)(2,1)}, u32[]{:S(2)}, u32[]{:S(2)}) async-start(bf16[2,4,64,1152]{3,1,0,2:T(4,128)(2,1)} %copy.64), calls=%async_computation.2 | async-start | bytes 2359296 | tf_op jit(solution)/shard_map/all_to_all | solution.py:114
  35.9 279.6 %reduce-scatter.26.cloned.1.call-start = ((), (), s32[]{:S(2)}) async-start(), calls=%async_computation.16 | async-start | bytes 26542080 | tf_op jit(solution)/shard_map/reduce_scatter | solution.py:197
  95.5 12.9 %copy-start.9 = (f32[2,4,4,16,1152]{4,3,1,2,0:T(8,128)}, f32[2,4,4,16,1152]{4,3,1,2,0:T(8,128)S(1)}, u32[]{:S(2)}) copy-start(f32[2,4,4,16,1152]{4,3,1,2,0:T(8,128)S(1)} %copy.65) | copy-start | bytes 7077892
  123.5 257.3 %reduce-scatter.20.cloned.1.call-start = ((), (), s32[]{:S(2)}) async-start(), calls=%async_computation.13 | async-start | bytes 6635520 | tf_op jit(solution)/shard_map/reduce_scatter | solution.py:195
  140.5 12.3 %copy-start.14 = (f32[2,4,4,16,1152]{4,3,2,1,0:T(8,128)S(1)}, f32[2,4,4,16,1152]{4,3,2,1,0:T(8,128)}, u32[]{:S(2)}) copy-start(f32[2,4,4,16,1152]{4,3,2,1,0:T(8,128)} %get-tuple-element.69) | copy-start | bytes 7077892
  163.9 367.6 %reduce-scatter.18.cloned.1.call-start = ((), (), s32[]{:S(2)}) async-start(), calls=%async_computation.12 | async-start | bytes 19906560 | tf_op jit(solution)/shard_map/reduce_scatter | solution.py:194
  205.6 11.1 %copy-start.4 = (f32[2,4,4,16,1152]{4,3,1,2,0:T(8,128)S(1)}, f32[2,4,4,16,1152]{4,3,1,2,0:T(8,128)}, u32[]{:S(2)}) copy-start(f32[2,4,4,16,1152]{4,3,1,2,0:T(8,128)} %copy-done.2) | copy-start | bytes 7077892
  228.6 13.3 %copy-start.11 = (f32[2,4,4,16,1152]{4,3,1,2,0:T(8,128)S(1)}, f32[2,4,4,16,1152]{4,3,1,2,0:T(8,128)}, u32[]{:S(2)}) copy-start(f32[2,4,4,16,1152]{4,3,1,2,0:T(8,128)} %copy-done.9) | copy-start | bytes 7077892
  228.6 13.3 %copy-start.42 = (f32[2,16]{1,0:T(2,128)S(1)}, f32[2,16]{1,0:T(2,128)}, u32[]{:S(2)}) copy-start(f32[2,16]{1,0:T(2,128)} %copy-done.41) | copy-start | bytes 388
  255.8 468.5 %reduce-scatter.22.cloned.1.call-start = ((), (), s32[]{:S(2)}) async-start(), calls=%async_computation.14 | async-start | bytes 26542080 | tf_op jit(solution)/shard_map/reduce_scatter | solution.py:196
  269.3 535.8 %reduce-scatter.28.cloned.1.call-start = ((), (), s32[]{:S(2)}) async-start(), calls=%async_computation.17 | async-start | bytes 4423680
  272.2 601.1 %reduce-scatter.34.cloned.1.call-start = ((), (), s32[]{:S(2)}) async-start(), calls=%async_computation.20 | async-start | bytes 7962624
  322.2 587.3 %reduce-scatter.32.cloned.1.call-start = ((), (), s32[]{:S(2)}) async-start(), calls=%async_computation.19 | async-start | bytes 1990656
  383.9 576.3 %reduce-scatter.30.cloned.1.call-start = ((), (), s32[]{:S(2)}) async-start(), calls=%async_computation.18 | async-start | bytes 4644864
  537.1 484.7 %reduce-scatter.24.cloned.1.call-start = ((), (), s32[]{:S(2)}) async-start(), calls=%async_computation.15 | async-start | bytes 5971968 | tf_op jit(solution)/shard_map/reduce_scatter | solution.py:207
  729.0 78.1 %collective-permute-start = (bf16[2,4,16,1152]{3,2,1,0:T(8,128)(2,1)S(1)}, bf16[2,4,16,1152]{3,2,1,0:T(8,128)(2,1)}, u32[]{:S(2)}, u32[]{:S(2)}) collective-permute-start(bf16[2,4,16,1152]{3,2,1,0:T(8,128)(2,1)S(1)} %get-tuple-element.82), channel_id=1, source_target_pairs={{0,1},{1,0},{2,3},{3,2},{4,5},{5,4},{6,7},{7,6},{8,9},{9,8},{10,11... | collective-permute-start | bytes 884744 | tf_op jit(solution)/shard_map/ppermute | solution.py:179
  730.4 78.5 %collective-permute-start.1 = (bf16[2,4,16,1152]{3,2,1,0:T(8,128)(2,1)S(1)}, bf16[2,4,16,1152]{3,2,1,0:T(8,128)(2,1)S(1)}, u32[]{:S(2)}, u32[]{:S(2)}) collective-permute-start(bf16[2,4,16,1152]{3,2,1,0:T(8,128)(2,1)S(1)} %get-tuple-element.81), channel_id=1, source_target_pairs={{0,2},{1,3},{2,0},{3,1},{4,6},{5,7},{6,4},{7,5},{8,10},{9,11},{10,... | collective-permute-start | bytes 884744 | tf_op jit(solution)/shard_map/ppermute | solution.py:179
  732.1 79.4 %all-to-all-start.1 = ((bf16[2,16,16,1152]{3,2,0,1:T(8,128)(2,1)}), bf16[2,16,16,1152]{3,2,0,1:T(8,128)(2,1)}, u32[]{:S(2)}, u32[]{:S(2)}) async-start(bf16[2,16,16,1152]{3,2,0,1:T(8,128)(2,1)} %copy.62), calls=%async_computation.1 | async-start | bytes 2359296 | tf_op jit(solution)/shard_map/all_to_all | solution.py:111
  778.4 31.2 %collective-permute-start.2 = (bf16[2,4,16,1152]{3,2,1,0:T(8,128)(2,1)S(1)}, bf16[2,4,16,1152]{3,2,1,0:T(8,128)(2,1)}, u32[]{:S(2)}, u32[]{:S(2)}) collective-permute-start(bf16[2,4,16,1152]{3,2,1,0:T(8,128)(2,1)S(1)} %get-tuple-element.80), channel_id=1, source_target_pairs={{0,3},{1,2},{2,1},{3,0},{4,7},{5,6},{6,5},{7,4},{8,11},{9,10},{10,... | collective-permute-start | bytes 884744 | tf_op jit(solution)/shard_map/ppermute | solution.py:179
  808.8 213.0 %copy-start.1 = (bf16[1152,1152]{1,0:T(8,128)(2,1)S(1)}, bf16[1152,1152]{1,0:T(8,128)(2,1)}, u32[]{:S(2)}) copy-start(bf16[1152,1152]{1,0:T(8,128)(2,1)} %param.17) | copy-start | bytes 7962628
  (40 other events, 173.9 us)
Sparse Core Ops, SparseCore 0:
  123.6 191.8 reduce-scatter.25
  318.7 61.9 reduce-scatter.19
  384.2 147.2 reduce-scatter.17
  534.4 189.9 reduce-scatter.21
  727.6 66.7 reduce-scatter.27
  796.7 76.6 reduce-scatter.33
  876.4 33.1 reduce-scatter.31
  912.5 47.6 reduce-scatter.29
  963.1 58.6 reduce-scatter.23
